TPU v7x, 32 devices: a whole 2x2x4 slice. The times are simulated.
32 devices in a mesh: blk: 4 (over y, x), dp: 8 (over z, core).
Axes of the slice: x: 2, y: 2, z: 4, core: 2. Of those that a mesh axis runs over, the one named last changes fastest.
Arguments:
- embed: bfloat16 [8192, 768], P(('blk', 'dp')), may hold values from -0.23925781 to 0.23925781
- log_scale: float32 [1], replicated, may hold values from 3 to 3.7
- bias: float32 [1], replicated, may hold values from -5.5 to -3.5
- partner_count: int32 [8192], P(('blk', 'dp')), may hold values from 1 to 4, as said below
- partner_owner: int32 [8192, 4], P(('blk', 'dp')), may hold values from 0 to 31, as said below
- partner_row: int32 [8192, 4], P(('blk', 'dp')), may hold values from 0 to 255
Outputs:
- embed_grad: bfloat16 [8192, 768], P(('blk', 'dp'))
Inputs may be any that keep to these rules, and one draw needn't show every extreme that they name: `partner_count`: 4 on some row of every device. `partner_owner`: every entry names a device other than the row's own device (devices numbered index along blk times 8 plus index along dp). Among the first partner_count entries of the rows of one device, no device is named more than 34 times, and some device exactly 34 times.
All inputs are finite; a program needn't handle non-finite values.
Results may differ from a plain program's by a relative error of at most 0.0065.
Values may be sent and summed in bfloat16 or wider, within the bound.
A program may use at most 64 MiB of HBM per device.

v0:
```python
import math
import jax
import jax.numpy as jnp
from jax import lax
from jax.sharding import PartitionSpec as P


def body(embed, log_scale, bias, partner_count, partner_owner, partner_row):
    rows_here, width = embed.shape
    most = partner_owner.shape[1]
    values = embed.astype(jnp.float32)
    inv_norm = lax.rsqrt(jnp.mean(values * values, axis=1, keepdims=True) + 1e-06)
    root_width = 1.0 / math.sqrt(width)
    unit_rows = (values * inv_norm * root_width).astype(jnp.bfloat16)
    logit_scale = jnp.exp(log_scale[0])
    logit_bias = bias[0]
    my_start = lax.axis_index("blk") * rows_here
    row_ids = my_start + jnp.arange(rows_here, dtype=jnp.int32)
    group = lax.all_gather(unit_rows, "blk", axis=0, tiled=True)
    scores = lax.dot_general(
        unit_rows, group, (((1,), (1,)), ((), ())), preferred_element_type=jnp.float32
    )
    columns = jnp.arange(group.shape[0], dtype=jnp.int32)
    weights = jnp.where(
        row_ids[:, None] == columns[None, :],
        jnp.float32(0.0),
        jax.nn.sigmoid(logit_bias + logit_scale * scores),
    )
    summed = jnp.dot(weights.astype(jnp.bfloat16), group, preferred_element_type=jnp.float32)
    neg_grad = 2.0 * logit_scale * summed
    n_all = lax.axis_size(("blk", "dp"))
    capacity = -(-(rows_here * most) // (n_all - 1))
    slots_all = n_all * capacity
    owner_flat = partner_owner.reshape(-1)
    live = (jnp.arange(most, dtype=jnp.int32)[None, :] < partner_count[:, None]).reshape(-1)
    one_hot = (
        (owner_flat[:, None] == jnp.arange(n_all, dtype=jnp.int32)[None, :]) & live[:, None]
    ).astype(jnp.int32)
    earlier = jnp.cumsum(one_hot, axis=0) - one_hot
    rank_in = jnp.sum(earlier * one_hot, axis=1)
    slot_of = jnp.where(live, owner_flat * capacity + rank_in, slots_all)
    send_index = (
        jnp.zeros((slots_all,), jnp.int32).at[slot_of].set(partner_row.reshape(-1), mode="drop")
    )
    recv_index = lax.all_to_all(
        send_index.reshape(n_all, capacity), ("blk", "dp"), split_axis=0, concat_axis=0, tiled=True
    ).reshape(-1)
    safe_slot = jnp.minimum(slot_of, slots_all - 1)
    asking = jnp.broadcast_to(unit_rows[:, None, :], (rows_here, most, width)).reshape(-1, width)
    replies = unit_rows[recv_index].reshape(n_all, capacity, width)
    arrived = lax.all_to_all(
        replies, ("blk", "dp"), split_axis=0, concat_axis=0, tiled=True
    ).reshape(-1, width)
    partner = arrived[safe_slot]
    scores = jnp.einsum("nd,nd->n", asking, partner, preferred_element_type=jnp.float32)
    weight = jnp.where(live, jax.nn.sigmoid(-(logit_bias + logit_scale * scores)), jnp.float32(0.0))
    own_terms = (
        (-logit_scale * weight[:, None] * partner.astype(jnp.float32))
        .astype(jnp.bfloat16)
        .astype(jnp.float32)
    )
    back_terms = (-logit_scale * weight[:, None] * asking.astype(jnp.float32)).astype(jnp.bfloat16)
    outgoing = jnp.zeros((slots_all, width), jnp.bfloat16).at[slot_of].set(back_terms, mode="drop")
    received = lax.all_to_all(
        outgoing.reshape(n_all, capacity, width),
        ("blk", "dp"),
        split_axis=0,
        concat_axis=0,
        tiled=True,
    ).reshape(-1, width)
    incoming = jax.ops.segment_sum(received.astype(jnp.float32), recv_index, num_segments=rows_here)
    row_grad = neg_grad + jnp.sum(own_terms.reshape(rows_here, most, width), axis=1) + incoming
    inner = jnp.sum(values * row_grad, axis=1, keepdims=True)
    result = root_width * inv_norm * (row_grad - values * inv_norm * inv_norm * inner / width)
    return result.astype(jnp.bfloat16)


def solution(mesh):
    return jax.shard_map(
        body,
        mesh=mesh,
        in_specs=(
            P(("blk", "dp"), None),
            P(),
            P(),
            P(("blk", "dp")),
            P(("blk", "dp"), None),
            P(("blk", "dp"), None),
        ),
        out_specs=P(("blk", "dp"), None),
        check_vma=False,
    )
```

profile of v0, /device:TPU:0, one launch (start us, length us, event | category | flops | bytes accessed | tf_op | source)
XLA Modules:
  0.0 187.4 jit_solution(1436901027829189112)
XLA Ops:
  6.5 0.8 lt.85
  7.3 0.8 iota_compare_fusion.4
  8.1 0.8 copy.15
  9.0 0.1 eq.45
  9.1 0.1 eq.41
  9.2 0.1 lt.81
  9.3 0.1 lt.82
  9.5 0.7 broadcast_multiply_fusion
  10.2 0.1 lt.84
  10.3 0.1 copy.17
  10.5 9.0 %reduce-window.6 = s32[32,8,128]{2,1,0:T(8,128)S(1)} reduce-window(s32[32,8,128]{2,1,0:T(8,128)S(1)} %fusion.34, s32[]{:T(128)} %constant.21.clone.1), window={size=1x1x128 pad=0_0x0_0x127_0}, to_apply=%region_1.2 | reduce-window | flops 4161536 | bytes 262148 | tf_op jit(solution)/shard_map/reduce-window
  19.5 0.1 slice.12
  19.6 0.1 copy.19
  19.8 0.1 copy.20
  19.8 0.1 broadcast_add_fusion
  19.9 0.1 copy.14
  20.1 0.1 mul.146
  20.2 0.0 copy-done.9
  20.2 0.1 copy.21
  20.4 0.1 reshape.233
  20.6 4.3 %scatter_custom_fusion = s32[1088]{0:T(1024)S(1)} fusion(s32[1024]{0:T(1024)S(1)} %bitcast.36, s32[1024]{0:T(1024)S(1)} %reshape.233, s32[]{:T(128)} %constant.21.clone.1), kind=kCustom, calls=%fused_computation.61 | custom fusion | bytes 4356 | tf_op jit(solution)/shard_map/scatter | solution.py:43
  24.9 0.7 all_to_all.12
  25.6 7.3 %all-to-all-start = ((s32[32,1,34]{2,1,0:T(1,128)}), s32[32,1,34]{2,1,0:T(1,128)S(1)}, u32[]{:S(2)}, u32[]{:S(2)}) async-start(s32[32,1,34]{2,1,0:T(1,128)} %all_to_all.12), calls=%async_computation | async-start | bytes 32768 | tf_op jit(solution)/shard_map/all_to_all | solution.py:45
  32.9 0.0 copy-done.3
  32.9 0.2 fusion.22
  33.1 0.6 broadcast_multiply_fusion.1
  33.7 0.2 fusion.16
  33.8 0.0 copy-start
  33.9 6.2 %all-to-all-done = s32[32,1,34]{2,1,0:T(1,128)S(1)} async-done(((s32[32,1,34]{2,1,0:T(1,128)}), s32[32,1,34]{2,1,0:T(1,128)S(1)}, u32[]{:S(2)}, u32[]{:S(2)}) %all-to-all-start) | async-done | bytes 4384 | tf_op jit(solution)/shard_map/all_to_all | solution.py:45
  40.1 0.6 broadcast.178
  40.6 0.7 reduce.9
  41.4 0.1 reshape.207
  41.5 4.5 %gather_fusion = bf16[1088,768]{1,0:T(8,128)(2,1)S(1)} fusion(bf16[256,768]{1,0:T(8,128)(2,1)S(1)} %fusion.16, s32[2048]{0:T(1024)S(1)} %pad_clamp_fusion), kind=kCustom, calls=%fused_computation | custom fusion | bytes 3346688 | tf_op jit(solution)/shard_map/gather | solution.py:50
  46.1 0.0 copy-done.7
  46.1 1.5 reshape.208
  47.6 3.5 %all-to-all-start.1 = ((bf16[32,34,768]{2,1,0:T(8,128)(2,1)}), bf16[32,34,768]{2,1,0:T(8,128)(2,1)}, u32[]{:S(2)}, u32[]{:S(2)}) async-start(bf16[32,34,768]{2,1,0:T(8,128)(2,1)} %reshape.208), calls=%async_computation.1 | async-start | bytes 3932160 | tf_op jit(solution)/shard_map/all_to_all | solution.py:51
  51.0 0.0 copy-done
  51.1 0.4 broadcast_in_dim.16
  51.5 0.4 reshape.204
  53.2 45.2 %all-to-all-done.1 = bf16[32,34,768]{2,1,0:T(8,128)(2,1)} async-done(((bf16[32,34,768]{2,1,0:T(8,128)(2,1)}), bf16[32,34,768]{2,1,0:T(8,128)(2,1)}, u32[]{:S(2)}, u32[]{:S(2)}) %all-to-all-start.1) | async-done | bytes 1671200 | tf_op jit(solution)/shard_map/all_to_all | solution.py:51
  98.4 2.5 %reshape.209 = bf16[1088,768]{1,0:T(8,128)(2,1)S(1)} reshape(bf16[32,34,768]{2,1,0:T(8,128)(2,1)} %all-to-all-done.1) | data formatting | bytes 3342336 | tf_op jit(solution)/shard_map/reshape | solution.py:53
  100.9 5.2 %gather_fusion.1 = bf16[1024,768]{1,0:T(8,128)(2,1)} fusion(bf16[1088,768]{1,0:T(8,128)(2,1)S(1)} %reshape.209, s32[1024]{0:T(1024)S(1)} %broadcast_clamp_fusion), kind=kCustom, calls=%fused_computation.1 | custom fusion | bytes 3149824 | tf_op jit(solution)/shard_map/gather | solution.py:54
  106.1 1.9 %fusion = f32[1024]{0:T(1024)S(1)} fusion(bf16[1024,768]{1,0:T(8,128)(2,1)S(1)} %reshape.204, bf16[1024,768]{1,0:T(8,128)(2,1)} %gather_fusion.1), kind=kLoop, calls=%fused_computation.7 | loop fusion | flops 3144704 | bytes 3149824 | tf_op jit(solution)/shard_map/nd,nd->n/dot_general | solution.py:55
  108.0 0.0 copy-start.5
  108.0 6.1 %scatter_custom_fusion.1 = bf16[1088,768]{1,0:T(8,128)(2,1)S(1)} fusion(s32[1024]{0:T(1024)S(1)} %bitcast.37, bf16[1024,768]{1,0:T(8,128)(2,1)S(1)} %reshape.204, f32[1024]{0:T(1024)S(1)} %select_multiply_fusion, bf16[]{:T(256)} %constant.9.clone.1), kind=kCustom, calls=%fused_computation.11 | custom fusion | flops 2359296 | bytes 3248130 | tf_op jit(solution)/shard_map/scatter | solution.py:63
  114.1 0.0 copy-done.5
  114.1 1.5 reshape.210
  115.6 2.8 %all-to-all-start.2 = ((bf16[32,34,768]{2,1,0:T(8,128)(2,1)}), bf16[32,34,768]{2,1,0:T(8,128)(2,1)S(1)}, u32[]{:S(2)}, u32[]{:S(2)}) async-start(bf16[32,34,768]{2,1,0:T(8,128)(2,1)} %reshape.210), calls=%async_computation.2 | async-start | bytes 3932160 | tf_op jit(solution)/shard_map/all_to_all | solution.py:64
  118.5 0.2 all-gather.2.cloned.1.call-start
  118.7 0.5 all-gather.2.cloned.1.call-update
  119.2 0.5 iota_add_fusion
  119.8 0.7 reshape.247
  120.5 1.5 mul.150
  121.9 0.0 copy-done.2
  121.9 2.0 %reshape.211 = f32[256,4,768]{2,1,0:T(4,128)} reshape(bf16[1024,768]{1,0:T(8,128)(2,1)S(1)} %copy-done.2) | data formatting | bytes 4718592 | tf_op jit(solution)/shard_map/convert_element_type | solution.py:58
  124.0 4.8 %convert_reduce_fusion = f32[256,768]{1,0:T(8,128)} fusion(f32[256,4,768]{2,1,0:T(4,128)} %reshape.211, f32[256,4]{1,0:T(8,128)} %mul.150), kind=kLoop, calls=%fused_computation.9 | loop fusion | flops 2949120 | bytes 3936256 | tf_op jit(solution)/shard_map/reduce_sum | solution.py:72
  128.8 32.2 %all-gather.2.cloned.1.call-done = bf16[1024,768]{1,0:T(8,128)(2,1)} async-done(((bf16[256,768]{1,0:T(8,128)(2,1)}), bf16[1024,768]{1,0:T(8,128)(2,1)}) %all-gather.2.cloned.1.call-update) | async-done | bytes 1572880 | tf_op jit(solution)/shard_map/all_gather | solution.py:19
  160.9 0.0 copy-done.1
  161.0 3.3 %fusion.10 = f32[256,768]{1,0:T(8,128)S(1)} fusion(f32[256,768]{1,0:T(8,128)} %convert_reduce_fusion, bf16[1024,768]{1,0:T(8,128)(2,1)} %all-gather.2.cloned.1.call-done, bf16[256,768]{1,0:T(8,128)(2,1)S(1)} %copy-done.1, f32[]{:T(128)} %bitcast, f32[]{:T(128)} %bitcast.28, s32[256]{0:T(256)S(1)} %copy-done.11, f32[]{:T(128)S(6)} %mul_shard_map.3), kind=kOutput, calls=%fused_computation.20 | convolution fusion | flops 807796736 | bytes 3539980 | tf_op jit(solution)/shard_map/dot_general | solution.py:29
  164.3 1.5 all-to-all-done.2
  165.9 1.9 %reshape.249 = f32[1088,768]{1,0:T(8,128)} reshape(bf16[32,34,768]{2,1,0:T(8,128)(2,1)S(1)} %all-to-all-done.2) | data formatting | bytes 5013504 | tf_op jit(solution)/shard_map/convert_element_type | solution.py:71
  167.8 11.6 %scatter_fusion = f32[256,768]{1,0:T(8,128)S(1)} fusion(f32[256,768]{1,0:T(8,128)S(1)} %fusion.10, s32[1088]{0:T(1024)S(1)} %copy-done.6, f32[1088,768]{1,0:T(8,128)} %reshape.249), kind=kCustom, calls=%fused_computation.4 | custom fusion | flops 835584 | bytes 10031360 | tf_op jit(solution)/shard_map/scatter-add | solution.py:71
  179.4 0.2 fusion.23
  179.5 1.0 fusion.21
  (28 shorter events, 0.3 us)
Async XLA Ops:
  6.5 13.7 %copy-start.9 = (s32[256,4]{0,1:T(4,128)S(1)}, s32[256,4]{0,1:T(4,128)}, u32[]{:S(2)}) copy-start(s32[256,4]{0,1:T(4,128)} %param.11) | copy-start | bytes 12292
  6.5 26.4 %copy-start.3 = (bf16[256,768]{1,0:T(8,128)(2,1)S(1)}, bf16[256,768]{1,0:T(8,128)(2,1)}, u32[]{:S(2)}) copy-start(bf16[256,768]{1,0:T(8,128)(2,1)} %param.6) | copy-start | bytes 1179652
  25.6 14.4 %all-to-all-start = ((s32[32,1,34]{2,1,0:T(1,128)}), s32[32,1,34]{2,1,0:T(1,128)S(1)}, u32[]{:S(2)}, u32[]{:S(2)}) async-start(s32[32,1,34]{2,1,0:T(1,128)} %all_to_all.12), calls=%async_computation | async-start | bytes 32768 | tf_op jit(solution)/shard_map/all_to_all | solution.py:45
  33.7 12.4 %copy-start.7 = (f32[256]{0:T(256)}, f32[256]{0:T(256)S(1)}, u32[]{:S(2)}) copy-start(f32[256]{0:T(256)S(1)} %get-tuple-element.8) | copy-start | bytes 3076
  33.8 17.2 %copy-start = (bf16[256,768]{1,0:T(8,128)(2,1)}, bf16[256,768]{1,0:T(8,128)(2,1)S(1)}, u32[]{:S(2)}) copy-start(bf16[256,768]{1,0:T(8,128)(2,1)S(1)} %fusion.16) | copy-start | bytes 1179652
  47.6 50.8 %all-to-all-start.1 = ((bf16[32,34,768]{2,1,0:T(8,128)(2,1)}), bf16[32,34,768]{2,1,0:T(8,128)(2,1)}, u32[]{:S(2)}, u32[]{:S(2)}) async-start(bf16[32,34,768]{2,1,0:T(8,128)(2,1)} %reshape.208), calls=%async_computation.1 | async-start | bytes 3932160 | tf_op jit(solution)/shard_map/all_to_all | solution.py:51
  108.0 6.1 %copy-start.5 = (f32[1024]{0:T(1024)}, f32[1024]{0:T(1024)S(1)}, u32[]{:S(2)}) copy-start(f32[1024]{0:T(1024)S(1)} %select_multiply_fusion) | copy-start | bytes 12292
  115.6 6.3 %copy-start.2 = (bf16[1024,768]{1,0:T(8,128)(2,1)S(1)}, bf16[1024,768]{1,0:T(8,128)(2,1)}, u32[]{:S(2)}) copy-start(bf16[1024,768]{1,0:T(8,128)(2,1)} %gather_fusion.1) | copy-start | bytes 4718596
  115.6 50.2 %all-to-all-start.2 = ((bf16[32,34,768]{2,1,0:T(8,128)(2,1)}), bf16[32,34,768]{2,1,0:T(8,128)(2,1)S(1)}, u32[]{:S(2)}, u32[]{:S(2)}) async-start(bf16[32,34,768]{2,1,0:T(8,128)(2,1)} %reshape.210), calls=%async_computation.2 | async-start | bytes 3932160 | tf_op jit(solution)/shard_map/all_to_all | solution.py:64
  118.5 42.5 %all-gather.2.cloned.1.call-start = ((), (), s32[]{:S(2)}) async-start(), calls=%async_computation.3 | async-start | bytes 1966080 | tf_op jit(solution)/shard_map/all_gather | solution.py:19
  124.0 37.0 %copy-start.1 = (bf16[256,768]{1,0:T(8,128)(2,1)S(1)}, bf16[256,768]{1,0:T(8,128)(2,1)}, u32[]{:S(2)}) copy-start(bf16[256,768]{1,0:T(8,128)(2,1)} %copy-done) | copy-start | bytes 1179652
  124.0 37.0 %copy-start.11 = (s32[256]{0:T(256)S(1)}, s32[256]{0:T(256)}, u32[]{:S(2)}) copy-start(s32[256]{0:T(256)} %iota_add_fusion) | copy-start | bytes 3076
  164.3 3.4 %copy-start.6 = (s32[1088]{0:T(1024)S(1)}, s32[1088]{0:T(1024)}, u32[]{:S(2)}) copy-start(s32[1088]{0:T(1024)} %reshape.247) | copy-start | bytes 13060
  167.8 11.6 %copy-start.4 = (bf16[256,768]{1,0:T(8,128)(2,1)S(1)}, bf16[256,768]{1,0:T(8,128)(2,1)}, u32[]{:S(2)}) copy-start(bf16[256,768]{1,0:T(8,128)(2,1)} %param.6) | copy-start | bytes 1179652
  167.8 11.8 %copy-start.8 = (f32[256]{0:T(256)S(1)}, f32[256]{0:T(256)}, u32[]{:S(2)}) copy-start(f32[256]{0:T(256)} %copy-done.7) | copy-start | bytes 3076
  167.8 11.8 %copy-start.10 = (f32[256]{0:T(256)S(1)}, f32[256]{0:T(256)}, u32[]{:S(2)}) copy-start(f32[256]{0:T(256)} %get-tuple-element.7) | copy-start | bytes 3076
Sparse Core Ops, SparseCore 0:
  121.2 39.7 all-gather.1
where the time goes:
time: 188 us; the launch traced here: 187 us
  waiting for transfers between devices  85.6 us (46%)
  other arithmetic  38.4 us (20%)
  local copies, waits for them, and re-layouts  31.1 us (17%)
  between operations  15.1 us (8%)
  starting transfers between devices  13.8 us (7%)
  matrix products  3.34 us (2%)
    all_to_all x1, waiting for transfers between devices, body(): lax.all_to_all(replies, ('blk', 'dp'), split_axis=0, concat_axis=0, tiled...  45.2 us
    all_gather x1, waiting for transfers between devices, body(): group = lax.all_gather(unit_rows, 'blk', axis=0, tiled=True)  32.2 us
    scatter-add x1, other arithmetic, body(): jax.ops.segment_sum(received.astype(jnp.float32), recv_index, num_segment...  11.6 us
    another operation x3, other arithmetic  9.15 us
    all_to_all x1, starting transfers between devices, body(): lax.all_to_all(send_index.reshape(n_all, capacity), ('blk', 'dp'), split_...  7.3 us
    all_to_all x1, waiting for transfers between devices, body(): lax.all_to_all(send_index.reshape(n_all, capacity), ('blk', 'dp'), split_...  6.2 us
    scatter x1, other arithmetic, body(): jnp.zeros((slots_all, width), jnp.bfloat16).at[slot_of]  6.08 us
    gather x1, local copies, waits for them, and re-layouts, body(): partner = arrived[safe_slot]  5.21 us
  transfers between devices with their start and end apart: 4, of which 4 were waited for; matrix products, arithmetic and copies ran while one was open for 8% of the time, Pallas kernels for 0%

commit v1 on v0

--- a/solution.py
+++ b/solution.py
@@ -16,7 +16,24 @@
     logit_bias = bias[0]
     my_start = lax.axis_index("blk") * rows_here
     row_ids = my_start + jnp.arange(rows_here, dtype=jnp.int32)
-    group = lax.all_gather(unit_rows, "blk", axis=0, tiled=True)
+    size, here, extent = (lax.axis_size("blk"), lax.axis_index("blk"), unit_rows.shape[0])
+    upward = [(i, (i + 1) % size) for i in range(size)]
+    left = [(i, (i - 1) % size) for i in range(size)]
+    out = jnp.zeros(
+        (*unit_rows.shape[:0], size * extent, *unit_rows.shape[0 + 1 :]), unit_rows.dtype
+    )
+    out = lax.dynamic_update_slice_in_dim(out, unit_rows, here * extent, axis=0)
+    from_left = from_right = unit_rows
+    half = size // 2
+    for step in range(1, half + 1):
+        from_left = lax.ppermute(from_left, "blk", upward)
+        out = lax.dynamic_update_slice_in_dim(out, from_left, (here - step) % size * extent, axis=0)
+        if step < size - half:
+            from_right = lax.ppermute(from_right, "blk", left)
+            out = lax.dynamic_update_slice_in_dim(
+                out, from_right, (here + step) % size * extent, axis=0
+            )
+    group = out
     scores = lax.dot_general(
         unit_rows, group, (((1,), (1,)), ((), ())), preferred_element_type=jnp.float32
     )

time: 188 us -> 195 us (1.037)
  between operations: 15.1 us -> 1.64 us
  waiting for transfers between devices: 85.6 us -> 95 us
  local copies, waits for them, and re-layouts: 31.1 us -> 38.6 us
  starting transfers between devices: 13.8 us -> 17.2 us
    ppermute x0 -> x3, waiting for transfers between devices: none -> 46.1 us  [the longest x2 36.1 us: body(): from_left = lax.ppermute(from_left, 'blk', upward)]
    all_gather x1 -> x0, waiting for transfers between devices: 32.2 us -> none  [body(): group = lax.all_gather(unit_rows, 'blk', axis=0, tiled=True)]
    dynamic_update_slice x0 -> x3, local copies, waits for them, and re-layouts: none -> 3.34 us  [the longest x1 1.77 us: body(): lax.dynamic_update_slice_in_dim(out, from_right, (here + step) % size * e...]
    ppermute x0 -> x3, starting transfers between devices: none -> 2.98 us  [the longest x2 1.63 us: body(): from_left = lax.ppermute(from_left, 'blk', upward)]
  transfers between devices with their start and end apart: 4 -> 6, of which waited for: 4 -> 5; matrix products, arithmetic and copies ran while one was open for 8% -> 9% of each run, Pallas kernels for 0% -> 0%
where the time goes in v1:
time: 195 us; the launch traced here: 194 us
  waiting for transfers between devices  95 us (49%)
  local copies, waits for them, and re-layouts  38.6 us (20%)
  other arithmetic  38.5 us (20%)
  starting transfers between devices  17.2 us (9%)
  matrix products  3.08 us (2%)
    all_to_all x1, waiting for transfers between devices, body(): lax.all_to_all(replies, ('blk', 'dp'), split_axis=0, concat_axis=0, tiled...  44.2 us
    ppermute x2, waiting for transfers between devices, body(): from_left = lax.ppermute(from_left, 'blk', upward)  36.1 us
    scatter-add x1, other arithmetic, body(): jax.ops.segment_sum(received.astype(jnp.float32), recv_index, num_segment...  11.6 us
    ppermute x1, waiting for transfers between devices, body(): from_right = lax.ppermute(from_right, 'blk', left)  9.96 us
    another operation x3, other arithmetic  9.15 us
    all_to_all x1, starting transfers between devices, body(): lax.all_to_all(send_index.reshape(n_all, capacity), ('blk', 'dp'), split_...  7.3 us
    scatter x1, other arithmetic, body(): jnp.zeros((slots_all, width), jnp.bfloat16).at[slot_of]  6.92 us
    gather x1, local copies, waits for them, and re-layouts, body(): partner = arrived[safe_slot]  5.27 us
  transfers between devices with their start and end apart: 6, of which 5 were waited for; matrix products, arithmetic and copies ran while one was open for 9% of the time, Pallas kernels for 0%

profile of v1, /device:TPU:0, one launch (start us, length us, event | category | flops | bytes accessed | tf_op | source)
XLA Modules:
  0.0 194.0 jit_solution(17585222091225125952)
XLA Ops:
  0.0 0.8 lt.118
  0.8 0.8 iota_compare_fusion.4
  1.6 0.8 copy.15
  2.4 0.1 eq.49
  2.5 0.1 eq.45
  2.7 0.1 lt.114
  2.8 0.1 lt.115
  2.9 0.7 broadcast_multiply_fusion
  3.6 0.1 lt.117
  3.8 0.1 copy.17
  3.9 9.0 %reduce-window.6 = s32[32,8,128]{2,1,0:T(8,128)S(1)} reduce-window(s32[32,8,128]{2,1,0:T(8,128)S(1)} %fusion.34, s32[]{:T(128)} %constant.63.clone.1), window={size=1x1x128 pad=0_0x0_0x127_0}, to_apply=%region_1.2 | reduce-window | flops 4161536 | bytes 262148 | tf_op jit(solution)/shard_map/reduce-window
  13.0 0.1 slice.12
  13.1 0.1 copy.19
  13.2 0.1 copy.20
  13.3 0.1 broadcast_add_fusion
  13.4 0.1 copy.14
  13.6 0.1 mul.159
  13.7 0.0 copy-done.3
  13.7 0.1 copy.21
  13.8 0.1 reshape.233
  14.0 4.3 %scatter_custom_fusion = s32[1088]{0:T(1024)S(1)} fusion(s32[1024]{0:T(1024)S(1)} %bitcast.36, s32[1024]{0:T(1024)S(1)} %reshape.233, s32[]{:T(128)} %constant.63.clone.1), kind=kCustom, calls=%fused_computation.61 | custom fusion | bytes 4356 | tf_op jit(solution)/shard_map/scatter | solution.py:60
  18.4 0.7 all_to_all.12
  19.1 7.3 %all-to-all-start = ((s32[32,1,34]{2,1,0:T(1,128)}), s32[32,1,34]{2,1,0:T(1,128)S(1)}, u32[]{:S(2)}, u32[]{:S(2)}) async-start(s32[32,1,34]{2,1,0:T(1,128)} %all_to_all.12), calls=%async_computation | async-start | bytes 32768 | tf_op jit(solution)/shard_map/all_to_all | solution.py:62
  26.4 0.0 copy-done.2
  26.4 0.2 fusion.22
  26.6 1.3 broadcast_in_dim.18
  27.8 0.9 constant_dynamic-update-slice_fusion.3
  28.7 4.7 %all-to-all-done = s32[32,1,34]{2,1,0:T(1,128)S(1)} async-done(((s32[32,1,34]{2,1,0:T(1,128)}), s32[32,1,34]{2,1,0:T(1,128)S(1)}, u32[]{:S(2)}, u32[]{:S(2)}) %all-to-all-start) | async-done | bytes 4384 | tf_op jit(solution)/shard_map/all_to_all | solution.py:62
  33.5 0.5 broadcast.181
  34.0 0.7 reduce.9
  34.7 0.1 reshape.207
  34.8 4.5 %gather_fusion = bf16[1088,768]{1,0:T(8,128)(2,1)S(1)} fusion(bf16[256,768]{1,0:T(8,128)(2,1)S(1)} %get-tuple-element.6, s32[2048]{0:T(1024)S(1)} %pad_clamp_fusion), kind=kCustom, calls=%fused_computation | custom fusion | bytes 3346688 | tf_op jit(solution)/shard_map/gather | solution.py:67
  39.3 1.6 reshape.208
  40.9 3.5 %all-to-all-start.1 = ((bf16[32,34,768]{2,1,0:T(8,128)(2,1)}), bf16[32,34,768]{2,1,0:T(8,128)(2,1)}, u32[]{:S(2)}, u32[]{:S(2)}) async-start(bf16[32,34,768]{2,1,0:T(8,128)(2,1)} %reshape.208), calls=%async_computation.1 | async-start | bytes 3932160 | tf_op jit(solution)/shard_map/all_to_all | solution.py:68
  44.4 0.4 broadcast_in_dim.19
  44.8 1.4 reshape.204
  47.5 44.2 %all-to-all-done.1 = bf16[32,34,768]{2,1,0:T(8,128)(2,1)} async-done(((bf16[32,34,768]{2,1,0:T(8,128)(2,1)}), bf16[32,34,768]{2,1,0:T(8,128)(2,1)}, u32[]{:S(2)}, u32[]{:S(2)}) %all-to-all-start.1) | async-done | bytes 1671200 | tf_op jit(solution)/shard_map/all_to_all | solution.py:68
  91.7 2.5 %reshape.209 = bf16[1088,768]{1,0:T(8,128)(2,1)S(1)} reshape(bf16[32,34,768]{2,1,0:T(8,128)(2,1)} %all-to-all-done.1) | data formatting | bytes 3342336 | tf_op jit(solution)/shard_map/reshape | solution.py:70
  94.2 5.3 %gather_fusion.1 = bf16[1024,768]{1,0:T(8,128)(2,1)} fusion(bf16[1088,768]{1,0:T(8,128)(2,1)S(1)} %reshape.209, s32[1024]{0:T(1024)S(1)} %broadcast_clamp_fusion), kind=kCustom, calls=%fused_computation.1 | custom fusion | bytes 3149824 | tf_op jit(solution)/shard_map/gather | solution.py:71
  99.5 2.5 %fusion = f32[1024]{0:T(1024)S(1)} fusion(bf16[1024,768]{1,0:T(8,128)(2,1)} %reshape.204, bf16[1024,768]{1,0:T(8,128)(2,1)} %gather_fusion.1), kind=kLoop, calls=%fused_computation.7 | loop fusion | flops 3144704 | bytes 3149824 | tf_op jit(solution)/shard_map/nd,nd->n/dot_general | solution.py:72
  102.0 0.0 copy-done
  102.0 6.9 %scatter_custom_fusion.1 = bf16[1088,768]{1,0:T(8,128)(2,1)} fusion(s32[1024]{0:T(1024)S(1)} %bitcast.37, bf16[1024,768]{1,0:T(8,128)(2,1)S(1)} %copy-done, f32[1024]{0:T(1024)S(1)} %select_multiply_fusion, bf16[]{:T(256)} %constant.62.clone.1), kind=kCustom, calls=%fused_computation.11 | custom fusion | flops 2359296 | bytes 3248130 | tf_op jit(solution)/shard_map/scatter | solution.py:80
  108.9 3.5 %reshape.210 = bf16[32,34,768]{2,1,0:T(8,128)(2,1)} reshape(bf16[1088,768]{1,0:T(8,128)(2,1)} %scatter_custom_fusion.1) | data formatting | bytes 3342336 | tf_op jit(solution)/shard_map/reshape | solution.py:82
  112.4 3.5 %all-to-all-start.2 = ((bf16[32,34,768]{2,1,0:T(8,128)(2,1)}), bf16[32,34,768]{2,1,0:T(8,128)(2,1)}, u32[]{:S(2)}, u32[]{:S(2)}) async-start(bf16[32,34,768]{2,1,0:T(8,128)(2,1)} %reshape.210), calls=%async_computation.2 | async-start | bytes 3932160 | tf_op jit(solution)/shard_map/all_to_all | solution.py:81
  115.8 0.0 copy-start.1
  115.9 1.6 collective-permute-start
  117.5 1.4 collective-permute-start.1
  118.8 26.8 %collective-permute-done = bf16[256,768]{1,0:T(8,128)(2,1)S(1)} collective-permute-done((bf16[256,768]{1,0:T(8,128)(2,1)S(1)}, bf16[256,768]{1,0:T(8,128)(2,1)S(1)}, u32[]{:S(2)}, u32[]{:S(2)}) %collective-permute-start) | collective-permute-done | bytes 393248 | tf_op jit(solution)/shard_map/ppermute | solution.py:29
  145.6 0.0 collective-permute-start.2
  145.6 0.1 reshape.247
  145.8 0.8 constant_dynamic-update-slice_fusion.2
  146.6 10.0 %collective-permute-done.1 = bf16[256,768]{1,0:T(8,128)(2,1)} collective-permute-done((bf16[256,768]{1,0:T(8,128)(2,1)S(1)}, bf16[256,768]{1,0:T(8,128)(2,1)}, u32[]{:S(2)}, u32[]{:S(2)}) %collective-permute-start.1) | collective-permute-done | bytes 393248 | tf_op jit(solution)/shard_map/ppermute | solution.py:32
  156.5 1.8 constant_dynamic-update-slice_fusion.1
  158.3 9.3 %collective-permute-done.2 = bf16[256,768]{1,0:T(8,128)(2,1)S(1)} collective-permute-done((bf16[256,768]{1,0:T(8,128)(2,1)S(1)}, bf16[256,768]{1,0:T(8,128)(2,1)S(1)}, u32[]{:S(2)}, u32[]{:S(2)}) %collective-permute-start.2) | collective-permute-done | bytes 393248 | tf_op jit(solution)/shard_map/ppermute | solution.py:29
  167.6 0.8 constant_dynamic-update-slice_fusion
  168.4 0.1 mul.163
  168.5 2.1 %reshape.211 = f32[256,4,768]{2,1,0:T(4,128)} reshape(bf16[1024,768]{1,0:T(8,128)(2,1)S(1)} %copy-done.1) | data formatting | bytes 4718592 | tf_op jit(solution)/shard_map/convert_element_type | solution.py:75
  170.6 3.8 %convert_reduce_fusion = f32[256,768]{1,0:T(8,128)S(1)} fusion(f32[256,4,768]{2,1,0:T(4,128)} %reshape.211, f32[256,4]{1,0:T(8,128)S(1)} %mul.163), kind=kLoop, calls=%fused_computation.9 | loop fusion | flops 2949120 | bytes 3936256 | tf_op jit(solution)/shard_map/reduce_sum | solution.py:89
  174.4 3.1 %fusion.10 = f32[256,768]{1,0:T(8,128)S(1)} fusion(f32[256,768]{1,0:T(8,128)S(1)} %convert_reduce_fusion, bf16[1024,768]{1,0:T(8,128)(2,1)} %constant_dynamic-update-slice_fusion, bf16[256,768]{1,0:T(8,128)(2,1)S(1)} %get-tuple-element.6, f32[]{:T(128)} %bitcast, f32[]{:T(128)} %bitcast.28, s32[256]{0:T(256)S(1)} %iota_add_fusion, f32[]{:T(128)S(6)} %mul_shard_map.3), kind=kOutput, calls=%fused_computation.20 | convolution fusion | flops 807796736 | bytes 3539980 | tf_op jit(solution)/shard_map/dot_general | solution.py:46
  177.5 0.0 all-to-all-done.2
  177.5 3.7 %reshape.249 = f32[1088,768]{1,0:T(8,128)} reshape(bf16[32,34,768]{2,1,0:T(8,128)(2,1)} %all-to-all-done.2) | data formatting | bytes 5013504 | tf_op jit(solution)/shard_map/convert_element_type | solution.py:88
  181.3 11.6 %scatter_fusion = f32[256,768]{1,0:T(8,128)S(1)} fusion(f32[256,768]{1,0:T(8,128)S(1)} %fusion.10, s32[1088]{0:T(1024)S(1)} %reshape.247, f32[1088,768]{1,0:T(8,128)} %reshape.249), kind=kCustom, calls=%fused_computation.4 | custom fusion | flops 835584 | bytes 10031360 | tf_op jit(solution)/shard_map/scatter-add | solution.py:88
  192.8 0.2 fusion.23
  193.0 1.0 fusion.21
  (19 shorter events, 0.3 us)
Async XLA Ops:
  0.0 13.7 %copy-start.3 = (s32[256,4]{0,1:T(4,128)S(1)}, s32[256,4]{0,1:T(4,128)}, u32[]{:S(2)}) copy-start(s32[256,4]{0,1:T(4,128)} %param.11) | copy-start | bytes 12292
  0.0 26.4 %copy-start.2 = (bf16[256,768]{1,0:T(8,128)(2,1)S(1)}, bf16[256,768]{1,0:T(8,128)(2,1)}, u32[]{:S(2)}) copy-start(bf16[256,768]{1,0:T(8,128)(2,1)} %param.6) | copy-start | bytes 1179652
  19.1 14.4 %all-to-all-start = ((s32[32,1,34]{2,1,0:T(1,128)}), s32[32,1,34]{2,1,0:T(1,128)S(1)}, u32[]{:S(2)}, u32[]{:S(2)}) async-start(s32[32,1,34]{2,1,0:T(1,128)} %all_to_all.12), calls=%async_computation | async-start | bytes 32768 | tf_op jit(solution)/shard_map/all_to_all | solution.py:62
  40.9 50.8 %all-to-all-start.1 = ((bf16[32,34,768]{2,1,0:T(8,128)(2,1)}), bf16[32,34,768]{2,1,0:T(8,128)(2,1)}, u32[]{:S(2)}, u32[]{:S(2)}) async-start(bf16[32,34,768]{2,1,0:T(8,128)(2,1)} %reshape.208), calls=%async_computation.1 | async-start | bytes 3932160 | tf_op jit(solution)/shard_map/all_to_all | solution.py:68
  99.5 2.5 %copy-start = (bf16[1024,768]{1,0:T(8,128)(2,1)S(1)}, bf16[1024,768]{1,0:T(8,128)(2,1)}, u32[]{:S(2)}) copy-start(bf16[1024,768]{1,0:T(8,128)(2,1)} %reshape.204) | copy-start | bytes 4718596
  112.4 65.1 %all-to-all-start.2 = ((bf16[32,34,768]{2,1,0:T(8,128)(2,1)}), bf16[32,34,768]{2,1,0:T(8,128)(2,1)}, u32[]{:S(2)}, u32[]{:S(2)}) async-start(bf16[32,34,768]{2,1,0:T(8,128)(2,1)} %reshape.210), calls=%async_computation.2 | async-start | bytes 3932160 | tf_op jit(solution)/shard_map/all_to_all | solution.py:81
  115.8 52.7 %copy-start.1 = (bf16[1024,768]{1,0:T(8,128)(2,1)S(1)}, bf16[1024,768]{1,0:T(8,128)(2,1)}, u32[]{:S(2)}) copy-start(bf16[1024,768]{1,0:T(8,128)(2,1)} %gather_fusion.1) | copy-start | bytes 4718596
  115.9 29.8 %collective-permute-start = (bf16[256,768]{1,0:T(8,128)(2,1)S(1)}, bf16[256,768]{1,0:T(8,128)(2,1)S(1)}, u32[]{:S(2)}, u32[]{:S(2)}) collective-permute-start(bf16[256,768]{1,0:T(8,128)(2,1)S(1)} %get-tuple-element.6), channel_id=1, source_target_pairs={{0,8},{8,16},{16,24},{24,0},{1,9},{9,17},{17,25},{25,1},{2,10},{10... | collective-permute-start | bytes 1179656 | tf_op jit(solution)/shard_map/ppermute | solution.py:29
  117.5 39.0 %collective-permute-start.1 = (bf16[256,768]{1,0:T(8,128)(2,1)S(1)}, bf16[256,768]{1,0:T(8,128)(2,1)}, u32[]{:S(2)}, u32[]{:S(2)}) collective-permute-start(bf16[256,768]{1,0:T(8,128)(2,1)S(1)} %get-tuple-element.6), channel_id=1, source_target_pairs={{0,24},{8,0},{16,8},{24,16},{1,25},{9,1},{17,9},{25,17},{2,26},{10... | collective-permute-start | bytes 1179656 | tf_op jit(solution)/shard_map/ppermute | solution.py:32
  145.6 22.0 %collective-permute-start.2 = (bf16[256,768]{1,0:T(8,128)(2,1)S(1)}, bf16[256,768]{1,0:T(8,128)(2,1)S(1)}, u32[]{:S(2)}, u32[]{:S(2)}) collective-permute-start(bf16[256,768]{1,0:T(8,128)(2,1)S(1)} %collective-permute-done), channel_id=1, source_target_pairs={{0,8},{8,16},{16,24},{24,0},{1,9},{9,17},{17,25},{25,1},{2,10},{10... | collective-permute-start | bytes 1179656 | tf_op jit(solution)/shard_map/ppermute | solution.py:29
